TPU v7x, 128 devices: a whole 4x4x4 slice. The times are simulated.
128 devices in a mesh: slab: 32 (over z, y, x_hi), chan: 4 (over x_lo, core).
Axes of the slice: x: 4 (x_hi: 2, x_lo: 2; x = x_hi * 2 + x_lo), y: 4, z: 4, core: 2. Of those that a mesh axis runs over, the one named last changes fastest.
Arguments:
- volume: bfloat16 [2, 128, 128, 32, 128], P(None, 'slab', 'chan'), may hold values from -6 to 6
- first_kernel: bfloat16 [3, 3, 3, 128, 128], P(None, None, None, None, 'chan'), may hold values from -0.109375 to 0.109375
- first_bias: float32 [128], P('chan'), may hold values from -3 to 3
- second_kernel: bfloat16 [3, 3, 3, 128, 128], P(None, None, None, 'chan'), may hold values from -0.109375 to 0.109375
- second_bias: float32 [128], P('chan'), may hold values from -3 to 3
Outputs:
- features_out: bfloat16 [2, 128, 128, 32, 128], P(None, 'slab', 'chan')
All inputs are finite; a program needn't handle non-finite values.
Results may differ from a plain program's by a relative error of at most 0.0046.
Values may be sent and summed in bfloat16 or wider, within the bound.
A program may use at most 128 MiB of HBM per device.

v0:
```python
import jax
import jax.numpy as jnp
from jax import lax
from jax.sharding import PartitionSpec as P

layout_spec = ("NDCHW", "DHWIO", "NDCHW")


def padded(shard, sides, width):
    for axis, dim in sides:
        size, length = (lax.axis_size(axis), shard.shape[dim])
        up = [(i, (i + 1) % size) for i in range(size - 1)]
        down = [(j, i) for i, j in up]
        last = lax.slice_in_dim(shard, length - width, length, axis=dim)
        initial = lax.slice_in_dim(shard, 0, width, axis=dim)
        before = lax.ppermute(last, axis, up)
        after = lax.ppermute(initial, axis, down)
        shard = jnp.concatenate([before, shard, after], axis=dim)
    return shard


def convolve(values_in, kernel):
    return lax.conv_general_dilated(
        values_in,
        kernel,
        (1, 1, 1),
        ((0, 0), (1, 1), (1, 1)),
        dimension_numbers=layout_spec,
        preferred_element_type=jnp.float32,
    )


def activate(summed, bias_row):
    return jax.nn.relu(summed + bias_row[None, None, :, None, None]).astype(jnp.bfloat16)


def body(volume, first_kernel, first_bias, second_kernel, second_bias):
    gathered = lax.all_gather(volume, "chan", axis=2, tiled=True)
    rimmed = padded(gathered, (("slab", 1),), 1)
    first_sum = convolve(rimmed, first_kernel)
    hidden = activate(first_sum, first_bias)
    hidden_rim = padded(hidden, (("slab", 1),), 1)
    partial_value = convolve(hidden_rim, second_kernel)
    second_sum = lax.psum_scatter(partial_value, "chan", scatter_dimension=2, tiled=True)
    return activate(second_sum, second_bias)


def solution(mesh):
    return jax.shard_map(
        body,
        mesh=mesh,
        in_specs=(
            P(None, "slab", "chan", None, None),
            P(None, None, None, None, "chan"),
            P("chan"),
            P(None, None, None, "chan", None),
            P("chan"),
        ),
        out_specs=P(None, "slab", "chan", None, None),
        check_vma=False,
    )
```

profile of v0, /device:TPU:98, one launch (start us, length us, event | category | flops | bytes accessed | tf_op | source)
XLA Modules:
  0.0 643.0 jit_solution(8899115111060957225)
XLA Ops:
  6.5 0.0 copy-start
  6.5 3.6 copy.33
  10.1 0.0 all-gather.2.cloned.1.call-update
  10.2 0.0 reduce-scatter.2.cloned.1.call-start
  10.2 81.1 %all-gather.2.cloned.1.call-done = bf16[2,4,128,32,128]{4,3,1,0,2:T(8,128)(2,1)} async-done(((bf16[2,4,32,32,128]{4,3,1,0,2:T(8,128)(2,1)}), bf16[2,4,128,32,128]{4,3,1,0,2:T(8,128)(2,1)}) %all-gather.2.cloned.1.call-update) | async-done | bytes 8388624 | tf_op jit(solution)/shard_map/all_gather | solution.py:38
  91.3 16.9 %copy.34 = bf16[2,4,128,32,128]{2,3,4,0,1:T(8,128)(2,1)} copy(bf16[2,4,128,32,128]{4,3,1,0,2:T(8,128)(2,1)} %all-gather.2.cloned.1.call-done) | data formatting | bytes 16777216 | tf_op jit(solution)/shard_map/all_gather | solution.py:38
  108.2 3.2 fusion.14
  111.3 4.1 collective-permute-start
  115.5 6.4 collective-permute-start.1
  121.9 44.5 %collective-permute-done = bf16[2,1,128,32,128]{2,3,4,0,1:T(8,128)(2,1)S(1)} collective-permute-done((bf16[2,1,128,32,128]{2,3,4,0,1:T(8,128)(2,1)S(1)}, bf16[2,1,128,32,128]{2,3,4,0,1:T(8,128)(2,1)S(1)}, u32[]{:S(2)}, u32[]{:S(2)}) %collective-permute-start) | collective-permute-done | bytes 2097184 | tf_op jit(solution)/shard_map/ppermute | solution.py:16
  166.3 42.9 %collective-permute-done.1 = bf16[2,1,128,32,128]{2,3,4,0,1:T(8,128)(2,1)S(1)} collective-permute-done((bf16[2,1,128,32,128]{2,3,4,0,1:T(8,128)(2,1)S(1)}, bf16[2,1,128,32,128]{2,3,4,0,1:T(8,128)(2,1)S(1)}, u32[]{:S(2)}, u32[]{:S(2)}) %collective-permute-start.1) | collective-permute-done | bytes 2097184 | tf_op jit(solution)/shard_map/ppermute | solution.py:17
  209.2 1.7 maximum_bitcast_fusion
  210.8 2.3 pad
  213.2 0.4 slice.26
  213.6 0.0 copy-start.5
  213.6 0.0 copy-start.6
  213.6 2.9 fusion.3
  216.6 82.8 %maximum_convert_fusion = bf16[4,32,16,17,32]{4,2,3,1,0:T(8,128)(2,1)S(1)} fusion(f32[32]{0:T(128)S(1)} %copy-done.5, pred[16,17]{0,1:T(8,128)(4,1)S(1)} %copy-done.6, bf16[3,3,3,128,32]{3,4,2,1,0:T(8,128)(2,1)} %param.6, bf16[6,128,32,2,8,19]{1,2,5,4,3,0:T(8,128)(2,1)S(1)} %fusion.3), kind=kOutput, calls=%fused_computation.4 | convolution fusion | flops 7544766464 | bytes 17392016 | tf_op jit(solution)/shard_map/conv_general_dilated | solution.py:23
  299.4 3.4 copy-done.3
  302.9 2.1 fusion.13
  305.0 9.3 %copy.40 = bf16[4,32,16,17,32]{4,1,3,2,0:T(8,128)(2,1)} copy(bf16[4,32,16,17,32]{4,2,3,1,0:T(8,128)(2,1)} %copy-done.3) | data formatting | bytes 4456448 | tf_op jit(solution)/shard_map/convert_element_type | solution.py:34
  314.2 2.2 copy.38
  316.5 1.7 slice_bitcast_fusion.3
  318.1 4.0 copy.39
  322.2 3.8 collective-permute-start.2
  326.0 0.6 copy.41
  326.6 0.4 slice_bitcast_fusion.2
  326.9 3.3 copy.42
  330.2 6.6 %collective-permute-start.3 = (bf16[2,1,32,32,128]{4,3,2,1,0:T(8,128)(2,1)}, bf16[2,1,32,32,128]{4,3,2,1,0:T(8,128)(2,1)}, u32[]{:S(2)}, u32[]{:S(2)}) collective-permute-start(bf16[2,1,32,32,128]{4,3,2,1,0:T(8,128)(2,1)} %copy.42), channel_id=1, source_target_pairs={{4,0},{8,4},{12,8},{16,12},{20,16},{24,20},{28,24},{32,28},{36,32}... | collective-permute-start | bytes 1572872 | tf_op jit(solution)/shard_map/ppermute | solution.py:17
  336.8 8.0 %slice_bitcast_fusion.1 = bf16[2,4,32,32,128]{2,3,4,0,1:T(8,128)(2,1)} fusion(bf16[4,32,2,136,32]{4,1,3,2,0:T(8,128)(2,1)} %bitcast.35), kind=kLoop, calls=%fused_computation.16 | loop fusion | bytes 4194304 | tf_op jit(solution)/shard_map/convert_element_type | solution.py:34
  344.8 0.0 collective-permute-done.2
  344.8 3.2 copy.43
  348.0 3.8 collective-permute-done.3
  351.8 5.2 copy.44
  357.0 10.6 %maximum_bitcast_fusion.1 = bf16[6,32,32,2,128]{1,2,4,3,0:T(8,128)(2,1)} fusion(bf16[2,1,32,32,128]{2,3,4,0,1:T(8,128)(2,1)} %copy.44, bf16[2,4,32,32,128]{2,3,4,0,1:T(8,128)(2,1)} %slice_bitcast_fusion.1, bf16[2,1,32,32,128]{2,3,4,0,1:T(8,128)(2,1)S(1)} %copy.43), kind=kLoop, calls=%fused_computation.14 | loop fusion | flops 3145728 | bytes 6291456 | tf_op jit(solution)/shard_map/concatenate | solution.py:18
  367.6 16.6 %copy.50 = bf16[6,32,32,2,128]{2,1,4,3,0:T(8,128)(2,1)} copy(bf16[6,32,32,2,128]{1,2,4,3,0:T(8,128)(2,1)} %maximum_bitcast_fusion.1) | data formatting | bytes 6291456
  384.2 7.0 %pad.2.clone = bf16[6,32,32,2,136]{2,1,4,3,0:T(8,128)(2,1)S(1)} pad(bf16[6,32,32,2,128]{2,1,4,3,0:T(8,128)(2,1)} %copy.50, bf16[]{:T(256)} %constant.5), padding=0_0x0_0x0_0x0_0x1_7 | pad | bytes 6488066 | tf_op jit(solution)/shard_map/concatenate | solution.py:18
  391.2 0.4 slice.32
  391.7 7.3 %fusion.2 = bf16[6,32,32,2,8,19]{2,1,5,4,3,0:T(8,128)(2,1)} fusion(bf16[6,32,32,2,7,2]{2,1,5,4,3,0:T(8,128)(2,1)S(1)} %slice.32, bf16[6,32,32,2,8,17]{2,1,5,4,3,0:T(8,128)(2,1)S(1)} %bitcast.32), kind=kLoop, calls=%fused_computation.6 | loop fusion | flops 11206656 | bytes 7421952 | tf_op jit(solution)/shard_map/conv_general_dilated | solution.py:23
  398.9 21.0 %copy.46 = bf16[6,32,32,2,8,19]{1,4,3,5,2,0:T(8,128)(2,1)} copy(bf16[6,32,32,2,8,19]{2,1,5,4,3,0:T(8,128)(2,1)} %fusion.2) | data formatting | bytes 7471104 | tf_op jit(solution)/shard_map/conv_general_dilated | solution.py:23
  420.0 31.6 %broadcast_select_fusion = f32[4,32,16,17,128]{4,2,3,1,0:T(8,128)S(1)} fusion(pred[16,17]{0,1:T(8,128)(4,1)S(1)} %copy-done.6, bf16[3,3,3,32,128]{4,3,2,1,0:T(8,128)(2,1)S(1)} %copy-done, bf16[6,32,32,2,8,19]{1,4,3,5,2,0:T(8,128)(2,1)} %copy.46), kind=kOutput, calls=%fused_computation.15 | convolution fusion | flops 7544766464 | bytes 21782800 | tf_op jit(solution)/shard_map/conv_general_dilated | solution.py:23
  451.6 6.2 copy.47
  457.8 6.2 slice_bitcast_fusion
  464.0 20.9 %copy.48 = f32[2,4,128,32,128]{4,3,1,0,2:T(8,128)} copy(f32[2,4,128,32,128]{2,3,4,0,1:T(8,128)} %slice_bitcast_fusion) | data formatting | bytes 33554432 | tf_op jit(solution)/shard_map/conv_general_dilated | solution.py:23
  484.9 0.0 reduce-scatter.2.cloned.1.call-update
  485.0 146.3 %reduce-scatter.2.cloned.1.call-done = f32[2,4,32,32,128]{4,3,1,0,2:T(8,128)} async-done(((f32[2,4,128,32,128]{4,3,1,0,2:T(8,128)}), f32[2,4,32,32,128]{4,3,1,0,2:T(8,128)}) %reduce-scatter.2.cloned.1.call-update) | async-done | bytes 4194320 | tf_op jit(solution)/shard_map/reduce_scatter | solution.py:44
  631.3 2.9 maximum_convert_fusion.1
  634.2 1.8 copy.49
  (11 shorter events, 0.0 us)
Async XLA Ops:
  6.5 413.5 %copy-start = (bf16[3,3,3,32,128]{4,3,2,1,0:T(8,128)(2,1)S(1)}, bf16[3,3,3,32,128]{4,3,2,1,0:T(8,128)(2,1)}, u32[]{:S(2)}) copy-start(bf16[3,3,3,32,128]{4,3,2,1,0:T(8,128)(2,1)} %param.8) | copy-start | bytes 663556
  6.5 84.7 %all-gather.2.cloned.1.call-start = ((), (), s32[]{:S(2)}) async-start(), calls=%async_computation.1 | async-start | bytes 10485760 | tf_op jit(solution)/shard_map/all_gather | solution.py:38
  10.2 621.1 %reduce-scatter.2.cloned.1.call-start = ((), (), s32[]{:S(2)}) async-start(), calls=%async_computation.2 | async-start | bytes 20971520 | tf_op jit(solution)/shard_map/reduce_scatter | solution.py:44
  108.2 101.0 %copy-start.2 = (bf16[2,4,128,32,128]{2,3,4,0,1:T(8,128)(2,1)S(1)}, bf16[2,4,128,32,128]{2,3,4,0,1:T(8,128)(2,1)}, u32[]{:S(2)}) copy-start(bf16[2,4,128,32,128]{2,3,4,0,1:T(8,128)(2,1)} %copy.34) | copy-start | bytes 25165828
  111.3 55.0 %collective-permute-start = (bf16[2,1,128,32,128]{2,3,4,0,1:T(8,128)(2,1)S(1)}, bf16[2,1,128,32,128]{2,3,4,0,1:T(8,128)(2,1)S(1)}, u32[]{:S(2)}, u32[]{:S(2)}) collective-permute-start(bf16[2,1,128,32,128]{2,3,4,0,1:T(8,128)(2,1)S(1)} %get-tuple-element.7), channel_id=1, source_target_pairs={{0,4},{4,8},{8,12},{12,16},{16,20},{20,24},{24,28},{28,32},{32,36}... | collective-permute-start | bytes 6291464 | tf_op jit(solution)/shard_map/ppermute | solution.py:16
  115.5 93.7 %collective-permute-start.1 = (bf16[2,1,128,32,128]{2,3,4,0,1:T(8,128)(2,1)S(1)}, bf16[2,1,128,32,128]{2,3,4,0,1:T(8,128)(2,1)S(1)}, u32[]{:S(2)}, u32[]{:S(2)}) collective-permute-start(bf16[2,1,128,32,128]{2,3,4,0,1:T(8,128)(2,1)S(1)} %get-tuple-element.8), channel_id=1, source_target_pairs={{4,0},{8,4},{12,8},{16,12},{20,16},{24,20},{28,24},{32,28},{36,32}... | collective-permute-start | bytes 6291464 | tf_op jit(solution)/shard_map/ppermute | solution.py:17
  213.6 3.0 copy-start.5
  213.6 3.0 copy-start.6
  299.4 3.5 copy-start.3
  322.2 22.6 %collective-permute-start.2 = (bf16[2,1,32,32,128]{4,3,2,1,0:T(8,128)(2,1)S(1)}, bf16[2,1,32,32,128]{4,3,2,1,0:T(8,128)(2,1)S(1)}, u32[]{:S(2)}, u32[]{:S(2)}) collective-permute-start(bf16[2,1,32,32,128]{4,3,2,1,0:T(8,128)(2,1)S(1)} %copy.39), channel_id=1, source_target_pairs={{0,4},{4,8},{8,12},{12,16},{16,20},{20,24},{24,28},{28,32},{32,36}... | collective-permute-start | bytes 1572872 | tf_op jit(solution)/shard_map/ppermute | solution.py:16
  330.2 21.6 %collective-permute-start.3 = (bf16[2,1,32,32,128]{4,3,2,1,0:T(8,128)(2,1)}, bf16[2,1,32,32,128]{4,3,2,1,0:T(8,128)(2,1)}, u32[]{:S(2)}, u32[]{:S(2)}) collective-permute-start(bf16[2,1,32,32,128]{4,3,2,1,0:T(8,128)(2,1)} %copy.42), channel_id=1, source_target_pairs={{4,0},{8,4},{12,8},{16,12},{20,16},{24,20},{28,24},{32,28},{36,32}... | collective-permute-start | bytes 1572872 | tf_op jit(solution)/shard_map/ppermute | solution.py:17
  484.9 146.4 %copy-start.4 = (f32[32]{0:T(128)S(1)}, f32[32]{0:T(128)}, u32[]{:S(2)}) copy-start(f32[32]{0:T(128)} %param.9) | copy-start | bytes 388
  484.9 151.0 %copy-start.1 = (bf16[3,3,3,32,128]{4,3,2,1,0:T(8,128)(2,1)S(1)}, bf16[3,3,3,32,128]{4,3,2,1,0:T(8,128)(2,1)}, u32[]{:S(2)}) copy-start(bf16[3,3,3,32,128]{4,3,2,1,0:T(8,128)(2,1)} %param.8) | copy-start | bytes 663556
Sparse Core Ops, SparseCore 0:
  10.3 80.9 all-gather.1
  485.1 146.1 reduce-scatter.1
where the time goes:
time: 646 us; the launch traced here: 643 us
  waiting for transfers between devices  319 us (49%)
  local copies, waits for them, and re-layouts  150 us (23%)
  matrix products  114 us (18%)
  other arithmetic  25.3 us (4%)
  starting transfers between devices  20.9 us (3%)
  between operations  13.8 us (2%)
    reduce_scatter x1, waiting for transfers between devices, body(): lax.psum_scatter(partial_value, 'chan', scatter_dimension=2, tiled=True)  146 us
    conv_general_dilated x2, matrix products, convolve(): lax.conv_general_dilated(values_in, kernel, (1, 1, 1), ((0, 0), (1, 1), (...  114 us
    all_gather x1, waiting for transfers between devices, body(): gathered = lax.all_gather(volume, 'chan', axis=2, tiled=True)  81.1 us
    conv_general_dilated x6, local copies, waits for them, and re-layouts, convolve(): lax.conv_general_dilated(values_in, kernel, (1, 1, 1), ((0, 0), (1, 1), (...  55.2 us
    ppermute x2, waiting for transfers between devices, padded(): after = lax.ppermute(initial, axis, down)  46.7 us
    ppermute x2, waiting for transfers between devices, padded(): before = lax.ppermute(last, axis, up)  44.5 us
    convert_element_type x6, local copies, waits for them, and re-layouts, activate(): jax.nn.relu(summed + bias_row[None, None, :, None, None])  24 us
    unnamed x16, local copies, waits for them, and re-layouts  23.7 us
  transfers between devices with their start and end apart: 6, of which 5 were waited for; matrix products, arithmetic and copies ran while one was open for 2% of the time, Pallas kernels for 0%

commit v1 on v0

v1 whole, which is shorter than its diff:
```python
import jax
import jax.numpy as jnp
from jax import lax
from jax.experimental import pallas as pl
from jax.experimental.pallas import tpu as pltpu
from jax.sharding import PartitionSpec as P

MESH = pl.DeviceIdType.MESH
SLABS = 32
BF16 = jnp.bfloat16
F32 = jnp.float32
LAYERS = (0, 1, 2, 3)


def conv_rows(source, layer, row, weights, bias):
    taps = [
        jnp.concatenate([source[layer + a, row + c], source[layer + a, row + c + 1]], axis=1)
        for a in range(3)
        for c in range(3)
    ]
    sums = jnp.dot(weights, jnp.concatenate(taps, axis=0), preferred_element_type=F32)
    lane = lax.broadcasted_iota(jnp.int32, (128, 128), 1)
    outs = []
    for r in range(2):
        cols = slice(128 * r, 128 * r + 128)
        left = jnp.where(lane == 0, 0.0, pltpu.roll(sums[0:128, cols], 1, 1))
        right = jnp.where(lane == 127, 0.0, pltpu.roll(sums[256:384, cols], 127, 1))
        outs.append(jnp.maximum(sums[128:256, cols] + left + right + bias, 0.0).astype(BF16))
    return outs


def stacked(taps):
    return jnp.concatenate([taps[3 * j : 3 * j + 3].reshape(384, 128) for j in range(9)], axis=1)


def kernel(
    vol, w1_in, w2_in, bias_in, out,
    landed, given, shared, x, hid, res, back, final, w1, w2, w2t, bias,
    sem_vol, sem_w, w_send, w_recv, x_send, x_recv, t_send, t_recv, z_send, z_recv, o_send, o_recv, o_self, sem_out,
):
    s = lax.axis_index("slab")
    k = lax.axis_index("chan")
    core = lax.rem(k, 2)
    chip = k // 2
    other = 1 - core
    sib = 2 * chip + other
    across = 2 * (1 - chip) + core
    diag = 2 * (1 - chip) + other
    mine = lax.rem(chip + s, 2)
    theirs = 1 - mine
    up, down = lax.rem(s + 1, SLABS), lax.rem(s + SLABS - 1, SLABS)
    pair = s + 1 - 2 * lax.rem(s, 2)
    has_down, has_up = s > 0, s < SLABS - 1
    ch = pl.ds(pl.multiple_of(k * 32, 32), 32)
    near_ch = pl.ds(pl.multiple_of(chip * 64, 64), 64)
    far_ch = pl.ds(pl.multiple_of((1 - chip) * 64, 64), 64)

    def remote(src, dst, send, recv, slab, chan):
        return pltpu.make_async_remote_copy(
            src_ref=src, dst_ref=dst, send_sem=send, recv_sem=recv, device_id=(slab, chan), device_id_type=MESH
        )

    barrier = pltpu.get_barrier_semaphore()
    for slab, chan in ((s, sib), (s, across), (s, diag), (up, across), (down, across)):
        pl.semaphore_signal(barrier, inc=1, device_id=(slab, chan), device_id_type=MESH)

    vol_copy = {}
    for z in LAYERS:
        for which, b in ((1, theirs), (0, mine)):
            vol_copy[which, z] = pltpu.make_async_copy(vol.at[b, z], landed.at[which, z], sem_vol.at[which, z])
            vol_copy[which, z].start()
    gathers = ((bias_in, bias), (w1_in, w1), (w2_in, w2))
    own_w = []
    for n, (src, dst) in enumerate(gathers):
        own_w.append(pltpu.make_async_copy(src, dst.at[:, ch, :], sem_w.at[n]))
        own_w[n].start()

    edge = 18 * core
    blank = jnp.zeros((2, 128, 128), BF16)

    def blank_rows(i, carry):
        x[i, pl.ds(edge, 2)] = blank
        return carry

    lax.fori_loop(0, 8, blank_rows, 0)

    def blank_layer(ref, layer, rows):
        def row(i, carry):
            ref[layer, i] = jnp.zeros((128, 128), BF16)
            return carry

        lax.fori_loop(0, rows, row, 0)

    @pl.when(jnp.logical_not(has_down))
    def _():
        blank_layer(x, 1, 20)
        blank_layer(hid, 0, 18)

    @pl.when(jnp.logical_not(has_up))
    def _():
        blank_layer(x, 6, 20)
        blank_layer(hid, 5, 18)

    pl.semaphore_wait(barrier, 5)

    def w_copy(n, i, chan_from, slab, chan):
        ref = gathers[n][1]
        part = ref.at[:, pl.ds(pl.multiple_of(chan_from * 32, 32), 32), :]
        return remote(part, part, w_send.at[n, i], w_recv.at[n, i], slab, chan)

    def start_w(n):
        own_w[n].wait()
        w_copy(n, 0, k, s, sib).start()
        w_copy(n, 1, k, pair, across).start()

    def pass_w(n):
        w_copy(n, 1, across, pair, across).wait_recv()
        w_copy(n, 2, across, s, sib).start()

    def end_w(n):
        w_copy(n, 0, sib, s, sib).wait_recv()
        w_copy(n, 2, diag, s, sib).wait_recv()

    def x_copy(z, i):
        rows = pl.ds(2, 16)
        if i == 0:
            return remote(shared.at[z], x.at[z + 2, rows, ch, :], x_send.at[z, 0], x_recv.at[z, 0], s, sib)
        half, chan = ((core, across), (other, diag))[i - 1]
        return remote(
            given.at[z, pl.ds(half * 16, 16)], x.at[z + 2, rows, ch, :], x_send.at[z, i], x_recv.at[z, i], s, chan
        )

    def give(z):
        vol_copy[1, z].wait()
        given[z] = jnp.swapaxes(landed[1, z], 0, 1)
        x_copy(z, 1).start()
        x_copy(z, 2).start()
        vol_copy[0, z].wait()
        final[0] = jnp.swapaxes(landed[0, z], 0, 1)
        x[z + 2, 2:18, ch, :] = final[0, pl.ds(core * 16, 16)]
        shared[z] = final[0, pl.ds(other * 16, 16)]
        x_copy(z, 0).start()

    def z_copy(z, part):
        lands, slab = {0: (6, down), 1: (7, down), 2: (0, up), 3: (1, up)}[z]
        channels = (near_ch, far_ch)[part]
        return remote(
            x.at[z + 2, pl.ds(2, 16), channels, :], x.at[lands, pl.ds(2, 16), channels, :],
            z_send.at[z, part], z_recv.at[z, part], slab, across,
        )

    def send_z(z, part):
        @pl.when(has_down if z < 2 else has_up)
        def _():
            z_copy(z, part).start()

    def t_copy(layer):
        return remote(
            x.at[layer, pl.ds(16 - 14 * core, 2)], x.at[layer, pl.ds(18 * core, 2)],
            t_send.at[layer], t_recv.at[layer], s, sib,
        )

    for z in LAYERS:
        give(z)
        if z == 0:
            start_w(0)
            start_w(1)
    start_w(2)
    for z in LAYERS:
        x_copy(z, 0).wait_recv()
        if z < 2:
            send_z(z, 0)
        if z == 0:
            pass_w(0)
            pass_w(1)
        x_copy(z, 1).wait_recv()
        x_copy(z, 2).wait_recv()
        if z < 2:
            send_z(z, 1)
        t_copy(z + 2).start()
    for z in (3, 2):
        send_z(z, 0)
        send_z(z, 1)
    pass_w(2)
    for n in range(3):
        end_w(n)

    def turn(i, carry):
        w2t[i] = w2[i].T
        return carry

    lax.fori_loop(0, 27, turn, 0)

    def outer(z, has):
        lands = {0: 6, 1: 7, 2: 0, 3: 1}[z]

        @pl.when(has)
        def _():
            for part in range(2):
                z_copy(z, part).wait_recv()
            t_copy(lands).start()
            t_copy(lands).wait_recv()

    def o_copy(z, i):
        chan = (sib, across, diag)[i]
        theirs_ch = pl.ds(pl.multiple_of(chan * 32, 32), 32)
        return remote(
            res.at[z, :, theirs_ch, :], back.at[mine, z, pl.ds(core * 16, 16)],
            o_send.at[z, i], o_recv.at[z, i], s, chan,
        )

    def o_own(z):
        return pltpu.make_async_copy(res.at[z, :, ch, :], back.at[mine, z, pl.ds(core * 16, 16)], o_self.at[z])

    def step(j, carry):
        layer = jnp.where(j < 4, j + 2, 5 - j)
        z_out = jnp.where(j < 4, j, 5 - j)

        @pl.when(j == 0)
        def _():
            for i in range(2, 5):
                t_copy(i).wait_recv()

        @pl.when(j == 1)
        def _():
            t_copy(5).wait_recv()

        for step_at, z, has in ((2, 0, has_up), (3, 1, has_up), (4, 3, has_down), (5, 2, has_down)):

            @pl.when(j == step_at)
            def _():
                outer(z, has)

        inside = jnp.logical_and(jnp.logical_or(has_up, j != 3), jnp.logical_or(has_down, j != 5))

        @pl.when(inside)
        def _():
            weights = stacked(w1)
            b = bias[0]
            for row in range(0, 18, 2):
                hid[layer, row], hid[layer, row + 1] = conv_rows(x, layer, row, weights, b)
            hid[layer, 17 * core] = jnp.zeros((128, 128), BF16)

        @pl.when(j >= 2)
        def _():
            weights = stacked(w2t)
            b = bias[1]
            for row in range(0, 16, 2):
                res[z_out, row], res[z_out, row + 1] = conv_rows(hid, z_out, row, weights, b)
            for i in (1, 2, 0):
                o_copy(z_out, i).start()
            o_own(z_out).start()

        return carry

    lax.fori_loop(0, 6, step, 0)

    def out_copy(b, z):
        return pltpu.make_async_copy(final.at[b * 4 + z], out.at[b, z], sem_out.at[b, z])

    for z in (2, 3, 1, 0):
        o_own(z).wait()
        for i in range(3):
            o_copy(z, i).wait_recv()
        for b in range(2):
            final[b * 4 + z] = jnp.swapaxes(back[b, z], 0, 1)
            out_copy(b, z).start()

    for n in range(3):
        for i, chan_from, slab, chan in ((0, k, s, sib), (1, k, pair, across), (2, across, s, sib)):
            w_copy(n, i, chan_from, slab, chan).wait_send()
    for z in LAYERS:
        for i in range(3):
            x_copy(z, i).wait_send()
            o_copy(z, i).wait_send()
        t_copy(z + 2).wait_send()

        @pl.when(has_down if z < 2 else has_up)
        def _():
            z_copy(z, 0).wait_send()
            z_copy(z, 1).wait_send()

        @pl.when(has_up if z < 2 else has_down)
        def _():
            t_copy({0: 6, 1: 7, 2: 0, 3: 1}[z]).wait_send()

        for b in range(2):
            out_copy(b, z).wait()


def body(volume, first_kernel, first_bias, second_kernel, second_bias):
    w1 = jnp.transpose(first_kernel, (0, 1, 2, 4, 3)).reshape(27, 32, 128)
    w2 = second_kernel.reshape(27, 32, 128)
    bias = jnp.broadcast_to(jnp.stack([first_bias, second_bias])[:, :, None], (2, 32, 128))
    hbm = pl.BlockSpec(memory_space=pl.ANY)
    dma = pltpu.SemaphoreType.DMA
    return pl.pallas_call(
        kernel,
        out_shape=jax.ShapeDtypeStruct((2, 4, 32, 32, 128), BF16),
        in_specs=[hbm] * 4,
        out_specs=hbm,
        scratch_shapes=[
            pltpu.VMEM((2, 4, 32, 32, 128), BF16),
            pltpu.VMEM((4, 32, 32, 128), BF16),
            pltpu.VMEM((4, 16, 32, 128), BF16),
            pltpu.VMEM((8, 20, 128, 128), BF16),
            pltpu.VMEM((6, 18, 128, 128), BF16),
            pltpu.VMEM((4, 16, 128, 128), BF16),
            pltpu.VMEM((2, 4, 32, 32, 128), BF16),
            pltpu.VMEM((8, 32, 32, 128), BF16),
            pltpu.VMEM((27, 128, 128), BF16),
            pltpu.VMEM((27, 128, 128), BF16),
            pltpu.VMEM((27, 128, 128), BF16),
            pltpu.VMEM((2, 128, 128), F32),
            dma((2, 4)),
            dma((3,)),
            dma((3, 3)),
            dma((3, 3)),
            dma((4, 3)),
            dma((4, 3)),
            dma((8,)),
            dma((8,)),
            dma((4, 2)),
            dma((4, 2)),
            dma((4, 3)),
            dma((4, 3)),
            dma((4,)),
            dma((2, 4)),
        ],
        name="two_convolutions",
        cost_estimate=pl.CostEstimate(flops=20_000_000_000, bytes_accessed=8_000_000, transcendentals=0),
        compiler_params=pltpu.CompilerParams(
            collective_id=0, has_side_effects=True, vmem_limit_bytes=48 * 1024 * 1024
        ),
    )(volume, w1, w2, bias)


def solution(mesh):
    return jax.shard_map(
        body,
        mesh=mesh,
        in_specs=(
            P(None, "slab", "chan", None, None),
            P(None, None, None, None, "chan"),
            P("chan"),
            P(None, None, None, "chan", None),
            P("chan"),
        ),
        out_specs=P(None, "slab", "chan", None, None),
        check_vma=False,
    )
```

time: 646 us -> 82.4 us (0.13)
  waiting for transfers between devices: 319 us -> 0 us
  local copies, waits for them, and re-layouts: 150 us -> 4.86 us
  matrix products: 114 us -> 0 us
  Pallas kernels: 0 us -> 76.2 us
  other arithmetic: 25.3 us -> 0.68 us
  starting transfers between devices: 20.9 us -> 0 us
  between operations: 13.8 us -> 0.01 us
    reduce_scatter x1 -> x0, waiting for transfers between devices: 146 us -> none  [body(): lax.psum_scatter(partial_value, 'chan', scatter_dimension=2, tiled=True)]
    conv_general_dilated x2 -> x0, matrix products: 114 us -> none  [convolve(): lax.conv_general_dilated(values_in, kernel, (1, 1, 1), ((0, 0), (1, 1), (...]
    ppermute x4 -> x0, waiting for transfers between devices: 91.1 us -> none  [the longest x2 46.7 us: padded(): after = lax.ppermute(initial, axis, down)]
    all_gather x1 -> x0, waiting for transfers between devices: 81.1 us -> none  [body(): gathered = lax.all_gather(volume, 'chan', axis=2, tiled=True)]
    pallas_call x0 -> x1, Pallas kernels: none -> 76.2 us  [body(): pl.pallas_call(kernel, out_shape=jax.ShapeDtypeStruct((2, 4, 32, 32, 128)...]
    conv_general_dilated x6 -> x0, local copies, waits for them, and re-layouts: 55.2 us -> none  [convolve(): lax.conv_general_dilated(values_in, kernel, (1, 1, 1), ((0, 0), (1, 1), (...]
    convert_element_type x6 -> x0, local copies, waits for them, and re-layouts: 24 us -> none  [activate(): jax.nn.relu(summed + bias_row[None, None, :, None, None])]
    ppermute x4 -> x0, starting transfers between devices: 20.8 us -> none  [the longest x2 12.9 us: padded(): after = lax.ppermute(initial, axis, down)]
  transfers between devices with their start and end apart: 6 -> 0, of which waited for: 5 -> 0; matrix products, arithmetic and copies ran while one was open for 2% -> 0% of each run, Pallas kernels for 0% -> 0%
where the time goes in v1:
time: 82.4 us; the launch traced here: 81.8 us
  Pallas kernels  76.2 us (92%)
  local copies, waits for them, and re-layouts  4.86 us (6%)
    pallas_call x1, Pallas kernels, body(): pl.pallas_call(kernel, out_shape=jax.ShapeDtypeStruct((2, 4, 32, 32, 128)...  76.2 us
    unnamed x7, local copies, waits for them, and re-layouts  4.79 us

profile of v1, /device:TPU:98, one launch (start us, length us, event | category | flops | bytes accessed | tf_op | source)
XLA Modules:
  0.0 81.8 jit_solution(18314092434734036072)
XLA Ops:
  0.0 0.7 pad_maximum_fusion
  0.7 0.1 broadcast_in_dim.2.bias_in
  0.8 0.0 copy-start
  0.8 1.6 %copy-done = bf16[2,4,32,32,128]{4,3,2,1,0:T(8,128)(2,1)S(1)} copy-done((bf16[2,4,32,32,128]{4,3,2,1,0:T(8,128)(2,1)S(1)}, bf16[2,4,32,32,128]{4,3,2,1,0:T(8,128)(2,1)}, u32[]{:S(2)}) %copy-start) | copy-done | bytes 2097176
  2.4 0.0 copy-start.1
  2.4 0.9 %copy-done.1 = bf16[3,3,3,128,32]{3,4,2,1,0:T(8,128)(2,1)S(1)} copy-done((bf16[3,3,3,128,32]{3,4,2,1,0:T(8,128)(2,1)S(1)}, bf16[3,3,3,128,32]{3,4,2,1,0:T(8,128)(2,1)}, u32[]{:S(2)}) %copy-start.1) | copy-done | bytes 221208
  3.3 0.0 copy-start.2
  3.3 0.9 %copy-done.2 = bf16[3,3,3,32,128]{4,3,2,1,0:T(8,128)(2,1)S(1)} copy-done((bf16[3,3,3,32,128]{4,3,2,1,0:T(8,128)(2,1)S(1)}, bf16[3,3,3,32,128]{4,3,2,1,0:T(8,128)(2,1)}, u32[]{:S(2)}) %copy-start.2) | copy-done | bytes 221208
  4.2 76.2 %two_convolutions.1 = bf16[2,4,32,32,128]{4,3,2,1,0:T(8,128)(2,1)S(1)} custom-call(bf16[2,4,32,32,128]{4,3,2,1,0:T(8,128)(2,1)S(1)} %copy-done, bf16[27,32,128]{2,1,0:T(8,128)(2,1)S(1)} %bitcast.6, bf16[27,32,128]{2,1,0:T(8,128)(2,1)S(1)} %bitcast.7, f32[2,32,128]{2,1,0:T(8,128)S(1)} %broadcast_in_dim.2.bias_in), custom_call_target="tpu_custom_call" | custom-call | flops 20000000000 | bytes 8000000 | tf_op jit(solution)/shard_map/two_convolutions/pallas_call | solution.py:297
  80.4 1.3 %copy.7 = bf16[2,4,32,32,128]{4,3,2,1,0:T(8,128)(2,1)} copy(bf16[2,4,32,32,128]{4,3,2,1,0:T(8,128)(2,1)S(1)} %two_convolutions.1) | data formatting | bytes 4194304
Async XLA Ops:
  0.8 1.6 %copy-start = (bf16[2,4,32,32,128]{4,3,2,1,0:T(8,128)(2,1)S(1)}, bf16[2,4,32,32,128]{4,3,2,1,0:T(8,128)(2,1)}, u32[]{:S(2)}) copy-start(bf16[2,4,32,32,128]{4,3,2,1,0:T(8,128)(2,1)} %vol.1) | copy-start | bytes 6291460
  2.4 0.9 %copy-start.1 = (bf16[3,3,3,128,32]{3,4,2,1,0:T(8,128)(2,1)S(1)}, bf16[3,3,3,128,32]{3,4,2,1,0:T(8,128)(2,1)}, u32[]{:S(2)}) copy-start(bf16[3,3,3,128,32]{3,4,2,1,0:T(8,128)(2,1)} %param.6) | copy-start | bytes 663556
  3.3 0.9 %copy-start.2 = (bf16[3,3,3,32,128]{4,3,2,1,0:T(8,128)(2,1)S(1)}, bf16[3,3,3,32,128]{4,3,2,1,0:T(8,128)(2,1)}, u32[]{:S(2)}) copy-start(bf16[3,3,3,32,128]{4,3,2,1,0:T(8,128)(2,1)} %param.8) | copy-start | bytes 663556

commit v2 on v0

v2 whole, which is shorter than its diff:
```python
import jax
import jax.numpy as jnp
from jax import lax
from jax.experimental import pallas as pl
from jax.experimental.pallas import tpu as pltpu
from jax.sharding import PartitionSpec as P

MESH = pl.DeviceIdType.MESH
SLABS = 32
BF16 = jnp.bfloat16
F32 = jnp.float32
CHUNKS = ((0, 6), (6, 4), (10, 4), (14, 2))
HIDDEN = (
    ((0, 6), (6, 4), (10, 4), (14, 3)),
    ((0, 4), (4, 2), (6, 2), (8, 2), (10, 2), (12, 2), (14, 2), (16, 1)),
)


def conv_rows(source, layer, row, weights, bias):
    taps = [
        jnp.concatenate([source[layer + a, row + c], source[layer + a, row + c + 1]], axis=1)
        for a in range(3)
        for c in range(3)
    ]
    sums = jnp.dot(weights, jnp.concatenate(taps, axis=0), preferred_element_type=F32)
    lane = lax.broadcasted_iota(jnp.int32, (128, 128), 1)
    outs = []
    for r in range(2):
        cols = slice(128 * r, 128 * r + 128)
        left = jnp.where(lane == 0, 0.0, pltpu.roll(sums[0:128, cols], 1, 1))
        right = jnp.where(lane == 127, 0.0, pltpu.roll(sums[256:384, cols], 127, 1))
        outs.append(jnp.maximum(sums[128:256, cols] + left + right + bias, 0.0).astype(BF16))
    return outs


def stacked(taps, core):
    parts = []
    for a in range(3):
        for c in range(3):
            at = 9 * a + 3 * (c + (1 - core) * (2 - 2 * c))
            parts.append(taps[pl.ds(at, 3)].reshape(384, 128))
    return jnp.concatenate(parts, axis=1)


def halves(rows):
    return jnp.stack([rows[15 - d] for d in range(16)]), rows[16:]


def kernel(
    vol, w1_in, w2_in, b1_in, b2_in, out,
    landed, given, own, x, hid, res, back, final, w, w2t, rows8, bias, b1_s, b2_s, sem_b,
    sem_vol, sem_w, w_send, w_recv, b_send, b_recv, x_send, x_recv, s_send, s_recv, t_send, t_recv,
    near_send, near_recv, far_send, far_recv, h_send, h_recv,
    in_send, in_recv, out_send, out_recv, sem_out,
):
    s = lax.axis_index("slab")
    k = lax.axis_index("chan")
    core = lax.rem(k, 2)
    chip = k // 2
    other = 1 - core
    sib = 2 * chip + other
    across = 2 * (1 - chip) + core
    diag = 2 * (1 - chip) + other
    mine = lax.rem(chip + s, 2)
    theirs = 1 - mine
    up, down = lax.rem(s + 1, SLABS), lax.rem(s + SLABS - 1, SLABS)
    y = lax.rem(s // 2, 4)
    odd = lax.rem(s // 8, 2)
    twin = 8 * (1 - 2 * odd)
    pair = s + 1 - 2 * lax.rem(s, 2)
    has_down, has_up = s > 0, s < SLABS - 1

    def y_peer(m):
        return s + 2 * (lax.rem(y + m, 4) - y)

    def chans(chan):
        return pl.ds(pl.multiple_of(chan * 32, 32), 32)

    ch = chans(k)
    far_ch = pl.ds(pl.multiple_of((1 - chip) * 64, 64), 64)

    def remote(src, dst, send, recv, slab, chan):
        return pltpu.make_async_remote_copy(
            src_ref=src, dst_ref=dst, send_sem=send, recv_sem=recv, device_id=(slab, chan), device_id_type=MESH
        )

    w[27] = jnp.zeros((128, 128), BF16)
    w[55] = jnp.zeros((128, 128), BF16)
    barrier = pltpu.get_barrier_semaphore()
    peers = [(s, sib), (s, across), (s, diag), (up, across), (down, across), (up, diag), (down, diag)]
    peers += [(y_peer(m), k) for m in (1, 2, 3)] + [(y_peer(m) + twin, k) for m in range(4)]
    for slab, chan in peers:
        pl.semaphore_signal(barrier, inc=1, device_id=(slab, chan), device_id_type=MESH)

    def own_w(n):
        return pltpu.make_async_copy((w1_in, w2_in)[n], w.at[pl.ds(28 * n, 27), ch, :], sem_w.at[n])

    def b_load(n):
        return pltpu.make_async_copy((b1_in, b2_in)[n], (b1_s, b2_s)[n], sem_b.at[n])

    def vol_copy(which, z):
        return pltpu.make_async_copy(vol.at[(mine, theirs)[which], z], landed.at[which, z], sem_vol.at[which, z])

    for n in range(2):
        b_load(n).start()
        own_w(n).start()
    for which, z in ((1, 0), (1, 1), (1, 2), (1, 3), (0, 0), (0, 3), (0, 1), (0, 2)):
        vol_copy(which, z).start()

    def blank():
        def blank_rows(i, carry):
            x[i, 18:20] = jnp.zeros((2, 128, 128), BF16)
            hid[i, 17] = jnp.zeros((128, 128), BF16)
            return carry

        lax.fori_loop(0, 6, blank_rows, 0)

        def blank_layer(layer):
            def row(i, carry):
                x[layer, i] = jnp.zeros((128, 128), BF16)
                hid[layer, i] = jnp.zeros((128, 128), BF16)
                return carry

            lax.fori_loop(0, 18, row, 0)

        @pl.when(jnp.logical_not(has_down))
        def _():
            blank_layer(0)

        @pl.when(jnp.logical_not(has_up))
        def _():
            blank_layer(5)

    at_row = lax.broadcasted_iota(jnp.int32, (8, 128), 0)
    at_lane = lax.broadcasted_iota(jnp.int32, (8, 128), 1) - 32 * k
    for n in range(2):
        b_load(n).wait()
    tile = jnp.zeros((8, 128), F32)
    for i in range(32):
        value = jnp.where(at_row == 0, b1_s[i], b2_s[i])
        tile = jnp.where(jnp.logical_and(at_lane == i, at_row < 2), value, tile)
    rows8[k] = tile

    def keep(which, z):
        vol_copy(which, z).wait()
        to = (own, given)[which]
        to[0, z], to[1, z] = halves(jnp.swapaxes(landed[which, z], 0, 1))

    for which, z in ((1, 0), (1, 1), (1, 2), (1, 3), (0, 0), (0, 3)):
        keep(which, z)
    pl.semaphore_wait(barrier, len(peers))

    def w_part(n, chan_from, quarter=None):
        taps = pl.ds(28 * n, 28) if quarter is None else pl.ds(28 * n + 7 * quarter, 7)
        return w.at[taps, chans(chan_from), :]

    def w_copy(i, receives=False):
        if i < 2:
            part, slab, chan = w_part(i, sib if receives else k), s, sib
        elif i < 4:
            part, slab, chan = w_part(i - 2, diag if receives else across), s, sib
        elif i == 4:
            part, slab, chan = w_part(odd, across if receives else k, y), pair, across
        else:
            m = i - 4 if i < 8 else i - 8
            n = odd if i < 8 or not receives else 1 - odd
            slab = y_peer(m) if i < 8 else y_peer(m) + twin
            part, chan = w_part(n, across, lax.rem(y + 4 - m, 4) if receives else y), k
        return remote(part, part, w_send.at[i], w_recv.at[i], slab, chan)

    def b_copy(i, receives=False):
        chan = (sib, across, diag)[i]
        part = rows8.at[chan if receives else k]
        return remote(part, part, b_send.at[i], b_recv.at[i], s, chan)

    for i in range(3):
        b_copy(i).start()
    for n in range(2):
        own_w(n).wait()
    w_copy(4).start()

    def x_copy(q, i):
        row, rows = CHUNKS[q]
        half, chan = ((core, across), (other, diag))[i]
        return remote(
            given.at[half, :, pl.ds(row, rows)], x.at[pl.ds(1, 4), pl.ds(row + 2, rows), ch, :],
            x_send.at[q, i], x_recv.at[q, i], s, chan,
        )

    def s_copy():
        return remote(own.at[other], x.at[pl.ds(1, 4), pl.ds(2, 16), ch, :], s_send, s_recv, s, sib)

    ENDS = ((3, 0, up, has_up, has_down), (0, 5, down, has_down, has_up))

    def near_copy(way, i):
        z, lands, slab = ENDS[way][:3]
        half, chan = ((core, across), (other, diag))[i]
        return remote(
            own.at[half, z], x.at[lands, pl.ds(2, 16), ch, :], near_send.at[way, i], near_recv.at[way, i], slab, chan
        )

    def far_copy(way, q):
        z, lands, slab = ENDS[way][:3]
        row, rows = CHUNKS[q]
        return remote(
            x.at[z + 1, pl.ds(row + 2, rows), far_ch, :], x.at[lands, pl.ds(row + 2, rows), far_ch, :],
            far_send.at[way, q], far_recv.at[way, q], slab, across,
        )

    def h_copy(way, q):
        z, lands, slab = ENDS[way][:3]
        rows = pl.ds(*HIDDEN[way][q])
        return remote(hid.at[z + 1, rows], hid.at[lands, rows], h_send.at[way, q], h_recv.at[way, q], slab, across)

    def t_copy(group, i):
        layers = (pl.ds(1, 4), 0, 5)[group]
        return remote(x.at[layers, 2 + i], x.at[layers, 1 - i], t_send.at[group, i], t_recv.at[group, i], s, sib)

    def start_ways(copy, way, *at):
        @pl.when(ENDS[way][3])
        def _():
            copy(way, *at).start()

    for q in range(4):
        for i in range(2):
            x_copy(q, i).start()
    for way in (1, 0):
        for i in range(2):
            start_ways(near_copy, way, i)
    for n in range(2):
        w_copy(n).start()
    for z in (1, 2):
        keep(0, z)
    s_copy().start()
    for z in range(4):
        x[z + 1, 2:18, ch, :] = own[core, z]
    blank()

    w_copy(4, True).wait_recv()
    for i in range(5, 12):
        w_copy(i).start()
    for i in range(3):
        b_copy(i, True).wait_recv()
    both = rows8[0] + rows8[1] + rows8[2] + rows8[3]
    for n in range(2):
        bias[n] = jnp.broadcast_to(both[n : n + 1], (128, 128)).T
    for i in range(5, 12):
        w_copy(i, True).wait_recv()
    for n in range(2):
        w_copy(n + 2).start()

    def turn(i, carry):
        w2t[i] = w[28 + i].T
        return carry

    s_copy().wait_recv()

    def o_copy(inner, z, q, i):
        chan = (sib, across, diag)[i]
        if inner:
            z, rows = pl.ds(1, 2), pl.ds(pl.multiple_of(4 * q, 4), 4)
            sems = in_send.at[q, i], in_recv.at[q, i]
        else:
            rows = pl.ds(pl.multiple_of(2 * q, 2), 2)
            sems = out_send.at[z // 3, q, i], out_recv.at[z // 3, q, i]
        return remote(res.at[z, rows, chans(chan), :], back.at[mine, z, core, rows], *sems, s, chan)

    def first(layers, row):
        weights, b = stacked(w, core), bias[0]
        for z in layers:
            for r in row:
                hid[z + 1, r], hid[z + 1, r + 1] = conv_rows(x, z, r, weights, b)

    def second(layers, row):
        weights, b = stacked(w2t, core), bias[1]
        for z in layers:
            for r in row:
                res[z, r], res[z, r + 1] = conv_rows(hid, z, r, weights, b)

    def last_row(layers):
        for z in layers:
            hid[z + 1, 17] = jnp.zeros((128, 128), BF16)

    def step(j, carry):
        @pl.when(j < 4)
        def _():
            for q in range(4):

                @pl.when(j == q)
                def _():
                    for i in range(2):
                        x_copy(q, i).wait_recv()
                    for way in (1, 0):
                        start_ways(far_copy, way, q)
                    if q == 0:
                        for i in range(2):
                            t_copy(0, i).start()
                        for n in (0, 2):
                            w_copy(n, True).wait_recv()

            first((1, 2), (4 * j + 2, 4 * j + 4))

            @pl.when(j == 0)
            def _():
                for i in range(2):
                    t_copy(0, i).wait_recv()
                first((1, 2), (0,))
                for n in (1, 3):
                    w_copy(n, True).wait_recv()
                lax.fori_loop(0, 27, turn, 0)

            @pl.when(j == 3)
            def _():
                last_row((1, 2))

        @pl.when(j >= 1)
        def _():
            i = j - 1
            for q in range(4):

                @pl.when(i == q)
                def _():
                    for way in (1, 0):

                        @pl.when(ENDS[way][4])
                        def _():
                            if q == 0:
                                for n in range(2):
                                    near_copy(way, n).wait_recv()
                            far_copy(way, q).wait_recv()
                            if q == 0:
                                for n in range(2):
                                    t_copy(1 + way, n).start()

            first((3, 0), (4 * i + 2, 4 * i + 4))

            @pl.when(i == 0)
            def _():
                for way in (1, 0):

                    @pl.when(ENDS[way][4])
                    def _():
                        for n in range(2):
                            t_copy(1 + way, n).wait_recv()

                first((3, 0), (0,))

            @pl.when(i == 3)
            def _():
                last_row((3, 0))

            for q in range(4):

                @pl.when(i == q)
                def _():
                    start_ways(h_copy, 0, q)
                    if q == 3:
                        for n in range(8):
                            start_ways(h_copy, 1, n)

            second((1, 2), (4 * i, 4 * i + 2))
            for n in (1, 2, 0):
                o_copy(True, None, i, n).start()

        return carry

    lax.fori_loop(0, 5, step, 0)

    def out_copy(b, z):
        return pltpu.make_async_copy(final.at[b * 4 + z], out.at[b, z], sem_out.at[b, z])

    def finish(z):
        back[mine, z, core] = res[z, :, ch, :]
        for b in range(2):
            rows = [back[b, z, 0, 15 - d] for d in range(16)] + [back[b, z, 1, d] for d in range(16)]
            final[b * 4 + z] = jnp.swapaxes(jnp.stack(rows), 0, 1)
            out_copy(b, z).start()

    def last_step(j, carry):
        z = 3 * (j // 8)
        i = lax.rem(j, 8)
        for way in range(2):
            for q in range((4, 8)[way]):

                @pl.when(jnp.logical_and(j == (2 * q, 8 + q)[way], ENDS[way][4]))
                def _():
                    h_copy(way, q).wait_recv()

        second((z,), (2 * i,))
        for n in (1, 2, 0):
            o_copy(False, z, i, n).start()

        @pl.when(j == 7)
        def _():
            for q in range(4):
                for n in range(3):
                    o_copy(True, None, q, n).wait_recv()
            finish(1)
            finish(2)

        @pl.when(j == 13)
        def _():
            for q in range(8):
                for n in range(3):
                    o_copy(False, 0, q, n).wait_recv()
            finish(0)

        return carry

    lax.fori_loop(0, 16, last_step, 0)
    for q in range(8):
        for n in range(3):
            o_copy(False, 3, q, n).wait_recv()
    finish(3)

    for i in range(12):
        w_copy(i).wait_send()
    for i in range(3):
        b_copy(i).wait_send()
    s_copy().wait_send()
    for i in range(2):
        t_copy(0, i).wait_send()
    for way in range(2):

        @pl.when(ENDS[way][3])
        def _():
            for i in range(2):
                near_copy(way, i).wait_send()
            for q in range(4):
                far_copy(way, q).wait_send()
            for q in range((4, 8)[way]):
                h_copy(way, q).wait_send()

        @pl.when(ENDS[way][4])
        def _():
            for i in range(2):
                t_copy(1 + way, i).wait_send()

    for q in range(4):
        for i in range(2):
            x_copy(q, i).wait_send()
        for i in range(3):
            o_copy(True, None, q, i).wait_send()
    for q in range(8):
        for i in range(3):
            o_copy(False, 0, q, i).wait_send()
            o_copy(False, 3, q, i).wait_send()
    for z in range(4):
        for b in range(2):
            out_copy(b, z).wait()


def body(volume, first_kernel, first_bias, second_kernel, second_bias):
    w1 = jnp.transpose(first_kernel, (0, 1, 2, 4, 3)).reshape(27, 32, 128)
    w2 = second_kernel.reshape(27, 32, 128)
    dma = pltpu.SemaphoreType.DMA
    return pl.pallas_call(
        kernel,
        out_shape=jax.ShapeDtypeStruct((2, 4, 32, 32, 128), BF16),
        in_specs=[pl.BlockSpec(memory_space=pl.ANY)] * 3 + [pl.BlockSpec(memory_space=pl.ANY)] * 2,
        out_specs=pl.BlockSpec(memory_space=pl.ANY),
        scratch_shapes=[
            pltpu.VMEM((2, 4, 32, 32, 128), BF16),
            pltpu.VMEM((2, 4, 16, 32, 128), BF16),
            pltpu.VMEM((2, 4, 16, 32, 128), BF16),
            pltpu.VMEM((6, 20, 128, 128), BF16),
            pltpu.VMEM((6, 18, 128, 128), BF16),
            pltpu.VMEM((4, 16, 128, 128), BF16),
            pltpu.VMEM((2, 4, 2, 16, 32, 128), BF16),
            pltpu.VMEM((8, 32, 32, 128), BF16),
            pltpu.VMEM((56, 128, 128), BF16),
            pltpu.VMEM((27, 128, 128), BF16),
            pltpu.VMEM((4, 8, 128), F32),
            pltpu.VMEM((2, 128, 128), F32),
            pltpu.SMEM((32,), F32),
            pltpu.SMEM((32,), F32),
            dma((2,)),
            dma((2, 4)),
            dma((2,)),
            dma((12,)),
            dma((12,)),
            dma((3,)),
            dma((3,)),
            dma((4, 2)),
            dma((4, 2)),
            dma,
            dma,
            dma((3, 2)),
            dma((3, 2)),
            dma((2, 2)),
            dma((2, 2)),
            dma((2, 4)),
            dma((2, 4)),
            dma((2, 8)),
            dma((2, 8)),
            dma((4, 3)),
            dma((4, 3)),
            dma((2, 8, 3)),
            dma((2, 8, 3)),
            dma((2, 4)),
        ],
        name="two_convolutions",
        cost_estimate=pl.CostEstimate(flops=20_000_000_000, bytes_accessed=8_000_000, transcendentals=0),
        compiler_params=pltpu.CompilerParams(
            collective_id=0, has_side_effects=True, vmem_limit_bytes=60 * 1024 * 1024
        ),
    )(volume, w1, w2, first_bias, second_bias)


def solution(mesh):
    return jax.shard_map(
        body,
        mesh=mesh,
        in_specs=(
            P(None, "slab", "chan", None, None),
            P(None, None, None, None, "chan"),
            P("chan"),
            P(None, None, None, "chan", None),
            P("chan"),
        ),
        out_specs=P(None, "slab", "chan", None, None),
        check_vma=False,
    )
```

time: 646 us -> 72.9 us (0.11)
  waiting for transfers between devices: 319 us -> 0 us
  local copies, waits for them, and re-layouts: 150 us -> 3.27 us
  matrix products: 114 us -> 0 us
  Pallas kernels: 0 us -> 68.3 us
  other arithmetic: 25.3 us -> 0 us
  starting transfers between devices: 20.9 us -> 0 us
  between operations: 13.8 us -> 0.01 us
    reduce_scatter x1 -> x0, waiting for transfers between devices: 146 us -> none  [body(): lax.psum_scatter(partial_value, 'chan', scatter_dimension=2, tiled=True)]
    conv_general_dilated x2 -> x0, matrix products: 114 us -> none  [convolve(): lax.conv_general_dilated(values_in, kernel, (1, 1, 1), ((0, 0), (1, 1), (...]
    ppermute x4 -> x0, waiting for transfers between devices: 91.1 us -> none  [the longest x2 46.7 us: padded(): after = lax.ppermute(initial, axis, down)]
    all_gather x1 -> x0, waiting for transfers between devices: 81.1 us -> none  [body(): gathered = lax.all_gather(volume, 'chan', axis=2, tiled=True)]
    pallas_call x0 -> x1, Pallas kernels: none -> 68.3 us  [body(): pl.pallas_call(kernel, out_shape=jax.ShapeDtypeStruct((2, 4, 32, 32, 128)...]
    conv_general_dilated x6 -> x0, local copies, waits for them, and re-layouts: 55.2 us -> none  [convolve(): lax.conv_general_dilated(values_in, kernel, (1, 1, 1), ((0, 0), (1, 1), (...]
    convert_element_type x6 -> x0, local copies, waits for them, and re-layouts: 24 us -> none  [activate(): jax.nn.relu(summed + bias_row[None, None, :, None, None])]
    ppermute x4 -> x0, starting transfers between devices: 20.8 us -> none  [the longest x2 12.9 us: padded(): after = lax.ppermute(initial, axis, down)]
  transfers between devices with their start and end apart: 6 -> 0, of which waited for: 5 -> 0; matrix products, arithmetic and copies ran while one was open for 2% -> 0% of each run, Pallas kernels for 0% -> 0%
where the time goes in v2:
time: 72.9 us; the launch traced here: 71.6 us
  Pallas kernels  68.3 us (94%)
  local copies, waits for them, and re-layouts  3.27 us (4%)
    pallas_call x1, Pallas kernels, body(): pl.pallas_call(kernel, out_shape=jax.ShapeDtypeStruct((2, 4, 32, 32, 128)...  68.3 us
    unnamed x1, local copies, waits for them, and re-layouts  3.27 us

profile of v2, /device:TPU:98, one launch (start us, length us, event | category | flops | bytes accessed | tf_op | source)
XLA Modules:
  0.0 71.6 jit_solution(2731268332438969759)
XLA Ops:
  0.0 68.3 %two_convolutions.1 = bf16[2,4,32,32,128]{4,3,2,1,0:T(8,128)(2,1)} custom-call(bf16[2,4,32,32,128]{4,3,2,1,0:T(8,128)(2,1)} %vol.1, bf16[27,32,128]{2,1,0:T(8,128)(2,1)} %bitcast.4, bf16[27,32,128]{2,1,0:T(8,128)(2,1)} %bitcast.5, f32[32]{0:T(128)} %b1_in.1, f32[32]{0:T(128)} %b2_in.1), custom_call_target="tpu_custom_call" | custom-call | flops 20000000000 | bytes 8000000 | tf_op jit(solution)/shard_map/two_convolutions/pallas_call | solution.py:457
  68.3 3.3 %copy.7 = bf16[2,4,32,32,128]{4,3,2,1,0:T(8,128)(2,1)} copy(bf16[2,4,32,32,128]{4,3,2,1,0:T(8,128)(2,1)} %two_convolutions.1) | data formatting | bytes 4194304

commit v3 on v2

--- a/solution.py
+++ b/solution.py
@@ -47,8 +47,8 @@
 
 
 def kernel(
-    vol, w1_in, w2_in, b1_in, b2_in, out,
-    landed, given, own, x, hid, res, back, final, w, w2t, rows8, bias, b1_s, b2_s, sem_b,
+    vol, w1_in, w2_in, b1_in, b2_in, back,
+    landed, given, own, x, hid, res, w, w2t, rows8, bias, b1_s, b2_s, sem_b,
     sem_vol, sem_w, w_send, w_recv, b_send, b_recv, x_send, x_recv, s_send, s_recv, t_send, t_recv,
     near_send, near_recv, far_send, far_recv, h_send, h_recv,
     in_send, in_recv, out_send, out_recv, sem_out,
@@ -366,15 +366,8 @@
 
     lax.fori_loop(0, 5, step, 0)
 
-    def out_copy(b, z):
-        return pltpu.make_async_copy(final.at[b * 4 + z], out.at[b, z], sem_out.at[b, z])
-
-    def finish(z):
-        back[mine, z, core] = res[z, :, ch, :]
-        for b in range(2):
-            rows = [back[b, z, 0, 15 - d] for d in range(16)] + [back[b, z, 1, d] for d in range(16)]
-            final[b * 4 + z] = jnp.swapaxes(jnp.stack(rows), 0, 1)
-            out_copy(b, z).start()
+    def own_copy(z):
+        return pltpu.make_async_copy(res.at[z, :, ch, :], back.at[mine, z, core], sem_out.at[z])
 
     def last_step(j, carry):
         z = 3 * (j // 8)
@@ -395,23 +388,23 @@
             for q in range(4):
                 for n in range(3):
                     o_copy(True, None, q, n).wait_recv()
-            finish(1)
-            finish(2)
+            own_copy(1).start()
+            own_copy(2).start()
 
         @pl.when(j == 13)
         def _():
             for q in range(8):
                 for n in range(3):
                     o_copy(False, 0, q, n).wait_recv()
-            finish(0)
+            own_copy(0).start()
 
         return carry
 
     lax.fori_loop(0, 16, last_step, 0)
+    own_copy(3).start()
     for q in range(8):
         for n in range(3):
             o_copy(False, 3, q, n).wait_recv()
-    finish(3)
 
     for i in range(12):
         w_copy(i).wait_send()
@@ -446,17 +439,22 @@
             o_copy(False, 0, q, i).wait_send()
             o_copy(False, 3, q, i).wait_send()
     for z in range(4):
-        for b in range(2):
-            out_copy(b, z).wait()
+        own_copy(z).wait()
+
+
+def finish(back, out):
+    for z in range(4):
+        rows = [back[0, z, 0, 15 - d] for d in range(16)] + [back[0, z, 1, d] for d in range(16)]
+        out[0, z] = jnp.swapaxes(jnp.stack(rows), 0, 1)
 
 
 def body(volume, first_kernel, first_bias, second_kernel, second_bias):
     w1 = jnp.transpose(first_kernel, (0, 1, 2, 4, 3)).reshape(27, 32, 128)
     w2 = second_kernel.reshape(27, 32, 128)
     dma = pltpu.SemaphoreType.DMA
-    return pl.pallas_call(
+    back = pl.pallas_call(
         kernel,
-        out_shape=jax.ShapeDtypeStruct((2, 4, 32, 32, 128), BF16),
+        out_shape=jax.ShapeDtypeStruct((2, 4, 2, 16, 32, 128), BF16),
         in_specs=[pl.BlockSpec(memory_space=pl.ANY)] * 3 + [pl.BlockSpec(memory_space=pl.ANY)] * 2,
         out_specs=pl.BlockSpec(memory_space=pl.ANY),
         scratch_shapes=[
@@ -466,8 +464,6 @@
             pltpu.VMEM((6, 20, 128, 128), BF16),
             pltpu.VMEM((6, 18, 128, 128), BF16),
             pltpu.VMEM((4, 16, 128, 128), BF16),
-            pltpu.VMEM((2, 4, 2, 16, 32, 128), BF16),
-            pltpu.VMEM((8, 32, 32, 128), BF16),
             pltpu.VMEM((56, 128, 128), BF16),
             pltpu.VMEM((27, 128, 128), BF16),
             pltpu.VMEM((4, 8, 128), F32),
@@ -497,7 +493,7 @@
             dma((4, 3)),
             dma((2, 8, 3)),
             dma((2, 8, 3)),
-            dma((2, 4)),
+            dma((4,)),
         ],
         name="two_convolutions",
         cost_estimate=pl.CostEstimate(flops=20_000_000_000, bytes_accessed=8_000_000, transcendentals=0),
@@ -505,6 +501,15 @@
             collective_id=0, has_side_effects=True, vmem_limit_bytes=60 * 1024 * 1024
         ),
     )(volume, w1, w2, first_bias, second_bias)
+    return pl.pallas_call(
+        finish,
+        grid=(2, 1),
+        out_shape=jax.ShapeDtypeStruct((2, 4, 32, 32, 128), BF16),
+        in_specs=[pl.BlockSpec((1, 4, 2, 16, 32, 128), lambda b, z: (b, z, 0, 0, 0, 0))],
+        out_specs=pl.BlockSpec((1, 4, 32, 32, 128), lambda b, z: (b, z, 0, 0, 0)),
+        name="rows_to_channels",
+        compiler_params=pltpu.CompilerParams(vmem_limit_bytes=16 * 1024 * 1024),
+    )(back)
 
 
 def solution(mesh):

time: 72.9 us -> 72.2 us (level)
  local copies, waits for them, and re-layouts: 3.27 us -> 1.58 us
  Pallas kernels: 68.3 us -> 69.2 us
    unnamed x1 -> x2, local copies, waits for them, and re-layouts: 3.27 us -> 1.58 us
    pallas_call x1 -> x2, Pallas kernels: 68.3 us -> 69.2 us  [the longest x1 67.6 us: body(): pl.pallas_call(kernel, out_shape=jax.ShapeDtypeStruct((2, 4, 2, 16, 32, 1...]
where the time goes in v3:
time: 72.2 us; the launch traced here: 70.8 us
  Pallas kernels  69.2 us (96%)
  local copies, waits for them, and re-layouts  1.58 us (2%)
    pallas_call x1, Pallas kernels, body(): pl.pallas_call(kernel, out_shape=jax.ShapeDtypeStruct((2, 4, 2, 16, 32, 1...  67.6 us
    pallas_call x1, Pallas kernels, body(): pl.pallas_call(finish, grid=(2, 1), out_shape=jax.ShapeDtypeStruct((2, 4,...  1.64 us
    unnamed x2, local copies, waits for them, and re-layouts  1.58 us

profile of v3, /device:TPU:98, one launch (start us, length us, event | category | flops | bytes accessed | tf_op | source)
XLA Modules:
  0.0 70.8 jit_solution(5449410366070387998)
XLA Ops:
  0.0 67.6 %two_convolutions.1.back = bf16[2,4,2,16,32,128]{5,4,3,2,1,0:T(8,128)(2,1)} custom-call(bf16[2,4,32,32,128]{4,3,2,1,0:T(8,128)(2,1)} %vol.1, bf16[27,32,128]{2,1,0:T(8,128)(2,1)} %bitcast.4, bf16[27,32,128]{2,1,0:T(8,128)(2,1)} %bitcast.5, f32[32]{0:T(128)} %b1_in.1, f32[32]{0:T(128)} %b2_in.1), custom_call_target="tpu_custom_call" | custom-call | flops 20000000000 | bytes 8000000 | tf_op jit(solution)/shard_map/two_convolutions/pallas_call | solution.py:455
  67.6 0.0 copy-start
  67.6 1.6 %copy-done = bf16[2,4,2,16,32,128]{5,4,3,2,1,0:T(8,128)(2,1)S(1)} copy-done((bf16[2,4,2,16,32,128]{5,4,3,2,1,0:T(8,128)(2,1)S(1)}, bf16[2,4,2,16,32,128]{5,4,3,2,1,0:T(8,128)(2,1)}, u32[]{:S(2)}) %copy-start) | copy-done | bytes 2097176
  69.2 1.6 %rows_to_channels.1 = bf16[2,4,32,32,128]{4,3,2,1,0:T(8,128)(2,1)} custom-call(bf16[2,4,2,16,32,128]{5,4,3,2,1,0:T(8,128)(2,1)S(1)} %copy-done), custom_call_target="tpu_custom_call" | custom-call | tf_op jit(solution)/shard_map/rows_to_channels/pallas_call | solution.py:504
Async XLA Ops:
  67.6 1.6 %copy-start = (bf16[2,4,2,16,32,128]{5,4,3,2,1,0:T(8,128)(2,1)S(1)}, bf16[2,4,2,16,32,128]{5,4,3,2,1,0:T(8,128)(2,1)}, u32[]{:S(2)}) copy-start(bf16[2,4,2,16,32,128]{5,4,3,2,1,0:T(8,128)(2,1)} %two_convolutions.1.back) | copy-start | bytes 6291460

commit v4 on v3

--- a/solution.py
+++ b/solution.py
@@ -11,8 +11,8 @@
 F32 = jnp.float32
 CHUNKS = ((0, 6), (6, 4), (10, 4), (14, 2))
 HIDDEN = (
-    ((0, 6), (6, 4), (10, 4), (14, 3)),
-    ((0, 4), (4, 2), (6, 2), (8, 2), (10, 2), (12, 2), (14, 2), (16, 1)),
+    ((1, 5), (6, 4), (10, 4), (14, 3)),
+    ((1, 3), (4, 2), (6, 2), (8, 2), (10, 2), (12, 2), (14, 2), (16, 1)),
 )
 
 
@@ -49,7 +49,7 @@
 def kernel(
     vol, w1_in, w2_in, b1_in, b2_in, back,
     landed, given, own, x, hid, res, w, w2t, rows8, bias, b1_s, b2_s, sem_b,
-    sem_vol, sem_w, w_send, w_recv, b_send, b_recv, x_send, x_recv, s_send, s_recv, t_send, t_recv,
+    sem_vol, sem_w, w_send, w_recv, b_send, b_recv, x_send, x_recv, s_send, s_recv, t_send, t_recv, u_send, u_recv,
     near_send, near_recv, far_send, far_recv, h_send, h_recv,
     in_send, in_recv, out_send, out_recv, sem_out,
 ):
@@ -216,6 +216,10 @@
         layers = (pl.ds(1, 4), 0, 5)[group]
         return remote(x.at[layers, 2 + i], x.at[layers, 1 - i], t_send.at[group, i], t_recv.at[group, i], s, sib)
 
+    def u_copy(way):
+        lands = ENDS[way][1]
+        return remote(hid.at[lands, 1], hid.at[lands, 0], u_send.at[way], u_recv.at[way], s, sib)
+
     def start_ways(copy, way, *at):
         @pl.when(ENDS[way][3])
         def _():
@@ -378,6 +382,9 @@
                 @pl.when(jnp.logical_and(j == (2 * q, 8 + q)[way], ENDS[way][4]))
                 def _():
                     h_copy(way, q).wait_recv()
+                    if q == 0:
+                        u_copy(way).start()
+                        u_copy(way).wait_recv()
 
         second((z,), (2 * i,))
         for n in (1, 2, 0):
@@ -426,6 +433,7 @@
 
         @pl.when(ENDS[way][4])
         def _():
+            u_copy(way).wait_send()
             for i in range(2):
                 t_copy(1 + way, i).wait_send()
 
@@ -483,6 +491,8 @@
             dma,
             dma((3, 2)),
             dma((3, 2)),
+            dma((2,)),
+            dma((2,)),
             dma((2, 2)),
             dma((2, 2)),
             dma((2, 4)),

time: 72.2 us -> 70.8 us (0.981)
  Pallas kernels: 69.2 us -> 67.9 us
    pallas_call x1, Pallas kernels: 67.6 us -> 66.2 us  [body(): pl.pallas_call(kernel, out_shape=jax.ShapeDtypeStruct((2, 4, 2, 16, 32, 1...]
where the time goes in v4:
time: 70.8 us; the launch traced here: 69.5 us
  Pallas kernels  67.9 us (96%)
  local copies, waits for them, and re-layouts  1.58 us (2%)
    pallas_call x1, Pallas kernels, body(): pl.pallas_call(kernel, out_shape=jax.ShapeDtypeStruct((2, 4, 2, 16, 32, 1...  66.2 us
    pallas_call x1, Pallas kernels, body(): pl.pallas_call(finish, grid=(2, 1), out_shape=jax.ShapeDtypeStruct((2, 4,...  1.64 us
    unnamed x2, local copies, waits for them, and re-layouts  1.58 us

profile of v4, /device:TPU:98, one launch (start us, length us, event | category | flops | bytes accessed | tf_op | source)
XLA Modules:
  0.0 69.5 jit_solution(9688725994721622232)
XLA Ops:
  0.0 66.2 %two_convolutions.1.back = bf16[2,4,2,16,32,128]{5,4,3,2,1,0:T(8,128)(2,1)} custom-call(bf16[2,4,32,32,128]{4,3,2,1,0:T(8,128)(2,1)} %vol.1, bf16[27,32,128]{2,1,0:T(8,128)(2,1)} %bitcast.4, bf16[27,32,128]{2,1,0:T(8,128)(2,1)} %bitcast.5, f32[32]{0:T(128)} %b1_in.1, f32[32]{0:T(128)} %b2_in.1), custom_call_target="tpu_custom_call" | custom-call | flops 20000000000 | bytes 8000000 | tf_op jit(solution)/shard_map/two_convolutions/pallas_call | solution.py:463
  66.2 0.0 copy-start
  66.3 1.6 %copy-done = bf16[2,4,2,16,32,128]{5,4,3,2,1,0:T(8,128)(2,1)S(1)} copy-done((bf16[2,4,2,16,32,128]{5,4,3,2,1,0:T(8,128)(2,1)S(1)}, bf16[2,4,2,16,32,128]{5,4,3,2,1,0:T(8,128)(2,1)}, u32[]{:S(2)}) %copy-start) | copy-done | bytes 2097176
  67.8 1.6 %rows_to_channels.1 = bf16[2,4,32,32,128]{4,3,2,1,0:T(8,128)(2,1)} custom-call(bf16[2,4,2,16,32,128]{5,4,3,2,1,0:T(8,128)(2,1)S(1)} %copy-done), custom_call_target="tpu_custom_call" | custom-call | tf_op jit(solution)/shard_map/rows_to_channels/pallas_call | solution.py:514
Async XLA Ops:
  66.2 1.6 %copy-start = (bf16[2,4,2,16,32,128]{5,4,3,2,1,0:T(8,128)(2,1)S(1)}, bf16[2,4,2,16,32,128]{5,4,3,2,1,0:T(8,128)(2,1)}, u32[]{:S(2)}) copy-start(bf16[2,4,2,16,32,128]{5,4,3,2,1,0:T(8,128)(2,1)} %two_convolutions.1.back) | copy-start | bytes 6291460

commit v5 on v4

--- a/solution.py
+++ b/solution.py
@@ -358,9 +358,8 @@
                 @pl.when(i == q)
                 def _():
                     start_ways(h_copy, 0, q)
-                    if q == 3:
-                        for n in range(8):
-                            start_ways(h_copy, 1, n)
+                    for n in {2: range(3), 3: range(3, 8)}.get(q, ()):
+                        start_ways(h_copy, 1, n)
 
             second((1, 2), (4 * i, 4 * i + 2))
             for n in (1, 2, 0):

time: 70.8 us -> 72.1 us (1.018); the launches traced: 69.5 us -> 71.9 us
  Pallas kernels: 67.9 us -> 70.3 us
    pallas_call x1, Pallas kernels: 66.2 us -> 68.7 us  [body(): pl.pallas_call(kernel, out_shape=jax.ShapeDtypeStruct((2, 4, 2, 16, 32, 1...]
where the time goes in v5:
time: 72.1 us; the launch traced here: 71.9 us
  Pallas kernels  70.3 us (98%)
  local copies, waits for them, and re-layouts  1.58 us (2%)
    pallas_call x1, Pallas kernels, body(): pl.pallas_call(kernel, out_shape=jax.ShapeDtypeStruct((2, 4, 2, 16, 32, 1...  68.7 us
    pallas_call x1, Pallas kernels, body(): pl.pallas_call(finish, grid=(2, 1), out_shape=jax.ShapeDtypeStruct((2, 4,...  1.64 us
    unnamed x2, local copies, waits for them, and re-layouts  1.58 us

profile of v5, /device:TPU:98, one launch (start us, length us, event | category | flops | bytes accessed | tf_op | source)
XLA Modules:
  0.0 71.9 jit_solution(13620241834603670950)
XLA Ops:
  0.0 68.7 %two_convolutions.1.back = bf16[2,4,2,16,32,128]{5,4,3,2,1,0:T(8,128)(2,1)} custom-call(bf16[2,4,32,32,128]{4,3,2,1,0:T(8,128)(2,1)} %vol.1, bf16[27,32,128]{2,1,0:T(8,128)(2,1)} %bitcast.4, bf16[27,32,128]{2,1,0:T(8,128)(2,1)} %bitcast.5, f32[32]{0:T(128)} %b1_in.1, f32[32]{0:T(128)} %b2_in.1), custom_call_target="tpu_custom_call" | custom-call | flops 20000000000 | bytes 8000000 | tf_op jit(solution)/shard_map/two_convolutions/pallas_call | solution.py:462
  68.7 0.0 copy-start
  68.7 1.6 %copy-done = bf16[2,4,2,16,32,128]{5,4,3,2,1,0:T(8,128)(2,1)S(1)} copy-done((bf16[2,4,2,16,32,128]{5,4,3,2,1,0:T(8,128)(2,1)S(1)}, bf16[2,4,2,16,32,128]{5,4,3,2,1,0:T(8,128)(2,1)}, u32[]{:S(2)}) %copy-start) | copy-done | bytes 2097176
  70.3 1.6 %rows_to_channels.1 = bf16[2,4,32,32,128]{4,3,2,1,0:T(8,128)(2,1)} custom-call(bf16[2,4,2,16,32,128]{5,4,3,2,1,0:T(8,128)(2,1)S(1)} %copy-done), custom_call_target="tpu_custom_call" | custom-call | tf_op jit(solution)/shard_map/rows_to_channels/pallas_call | solution.py:513
Async XLA Ops:
  68.7 1.6 %copy-start = (bf16[2,4,2,16,32,128]{5,4,3,2,1,0:T(8,128)(2,1)S(1)}, bf16[2,4,2,16,32,128]{5,4,3,2,1,0:T(8,128)(2,1)}, u32[]{:S(2)}) copy-start(bf16[2,4,2,16,32,128]{5,4,3,2,1,0:T(8,128)(2,1)} %two_convolutions.1.back) | copy-start | bytes 6291460
